TPU v7x, 128 devices: a whole 4x4x4 slice. The times are simulated.
128 devices in a mesh: aux: 4 (over y_lo, core), pair: 32 (over z, y_hi, x).
Axes of the slice: x: 4, y: 4 (y_hi: 2, y_lo: 2; y = y_hi * 2 + y_lo), z: 4, core: 2. Of those that a mesh axis runs over, the one named last changes fastest.
Arguments:
- amplitudes: bfloat16 [65536, 512], P('pair', 'aux'), may hold values from -4 to 4
- coulomb: bfloat16 [65536, 512], P('pair'), may hold values from -12 to 12
- df_factors: bfloat16 [65536, 2048], P('pair', 'aux'), may hold values from -0.07861328 to 0.07861328
- thc_left: bfloat16 [512, 1536], P('pair', 'aux'), may hold values from -0.50390625 to 0.50390625
- thc_right: bfloat16 [512, 1536], P('pair', 'aux'), may hold values from -0.50390625 to 0.50390625
- occ_energy: float32 [128], P('pair'), may hold values from -2 to -0.5
- vir_energy: float32 [512], replicated, may hold values from 0.5 to 3
- pivot_energy: float32 [1], replicated, may hold values from -2 to -0.5
Outputs:
- updated: bfloat16 [65536, 512], P('pair', 'aux')
All inputs are finite; a program needn't handle non-finite values.
Results may differ from a plain program's by a relative error of at most 0.0051.
Values may be sent and summed in bfloat16 or wider, within the bound.
A program may use at most 64 MiB of HBM per device.

v0:
```python
import jax
import jax.numpy as jnp
from jax import lax
from jax.sharding import PartitionSpec as P

ITERS = 2


def per_device(
    amplitudes, coulomb, df_factors, thc_left, thc_right, occ_energy, vir_energy, pivot_energy
):
    column_index = lax.axis_index("aux")
    width = amplitudes.shape[1]
    rows = amplitudes.shape[0]
    nvirt = vir_energy.shape[0]
    nocc_local = rows // nvirt
    denom_full = (
        vir_energy[None, :, None]
        + vir_energy[None, None, :]
        - occ_energy[:, None, None]
        - pivot_energy[0]
    ).reshape(rows, nvirt)
    local = amplitudes
    whole = None
    for step in range(ITERS):
        whole = lax.all_gather(local, "aux", axis=1, tiled=True)
        left, right = (
            lax.all_gather(thc_left, "pair", axis=0, tiled=True),
            lax.all_gather(thc_right, "pair", axis=0, tiled=True),
        )
        gram = lax.dot_general(
            df_factors, whole, (((0,), (0,)), ((), ())), preferred_element_type=jnp.float32
        )
        gram = lax.psum(gram, "pair").astype(jnp.bfloat16)
        proj = jnp.dot(whole, right, preferred_element_type=jnp.float32).reshape(
            nocc_local, nvirt, right.shape[1]
        )
        middle = jnp.sum(proj * left.astype(jnp.float32)[None], axis=1)
        weighted = (
            (left.astype(jnp.float32)[None] * middle[:, None, :])
            .astype(jnp.bfloat16)
            .reshape(rows, right.shape[1])
        )
        ladder = lax.dot_general(
            weighted, right, (((1,), (1,)), ((), ())), preferred_element_type=jnp.float32
        )
        cycle = jnp.dot(df_factors, gram, preferred_element_type=jnp.float32)
        part = cycle + ladder
        share = lax.psum_scatter(part, "aux", scatter_dimension=1, tiled=True)
        coulomb_block = lax.dynamic_slice_in_dim(coulomb, column_index * width, width, 1)
        denom_block = lax.dynamic_slice_in_dim(denom_full, column_index * width, width, 1)
        local = ((coulomb_block.astype(jnp.float32) + share) / denom_block).astype(jnp.bfloat16)
        whole = None
    return local


def solution(mesh):
    in_specs = (
        P("pair", "aux"),
        P("pair", None),
        P("pair", "aux"),
        P("pair", "aux"),
        P("pair", "aux"),
        P("pair"),
        P(),
        P(),
    )
    out_specs = P("pair", "aux")
    return jax.shard_map(
        per_device, mesh=mesh, in_specs=in_specs, out_specs=out_specs, check_vma=False
    )
```

profile of v0, /device:TPU:1, one launch (start us, length us, event | category | flops | bytes accessed | tf_op | source)
XLA Modules:
  0.0 727.8 jit_solution(6331696356727031182)
XLA Ops:
  6.5 0.7 all-gather.3.cloned.1.call-update
  7.3 0.0 reduce-scatter.3.cloned.1.call-start
  7.3 85.5 %all_gather.15 = bf16[512,384]{1,0:T(8,128)(2,1)S(1)} all-gather(bf16[16,384]{1,0:T(8,128)(2,1)} %param.11), channel_id=1, replica_groups=mesh['aux'=4,'pair'=32] {'pair'}, dimensions={0}, use_global_device_ids=true | all-gather | bytes 405504 | tf_op jit(solution)/shard_map/all_gather | solution.py:28
  92.8 0.1 convert_element_type.38
  92.9 75.5 %all_gather.16 = bf16[512,384]{1,0:T(8,128)(2,1)S(1)} all-gather(bf16[16,384]{1,0:T(8,128)(2,1)S(1)} %copy-done.6), channel_id=1, replica_groups=mesh['aux'=4,'pair'=32] {'pair'}, dimensions={0}, use_global_device_ids=true | all-gather | bytes 405504 | tf_op jit(solution)/shard_map/all_gather | solution.py:29
  168.3 3.0 multiply_reduce_fusion.1
  171.3 1.5 multiply_convert_fusion.1
  172.8 2.3 fusion.9
  175.1 162.7 %all-reduce.2 = bf16[512,512]{1,0:T(8,128)(2,1)} all-reduce(f32[512,512]{1,0:T(8,128)} %fusion.9), channel_id=1, replica_groups=mesh['aux'=4,'pair'=32] {'pair'}, use_global_device_ids=true, to_apply=%region_0.0 | all-reduce | flops 262144 | bytes 1572864 | tf_op jit(solution)/shard_map/psum | solution.py:34
  337.7 2.5 fusion.11
  340.2 3.3 bitcast_add_fusion.1
  343.6 0.0 all-gather.5.cloned.1.call-start
  343.6 1.9 constant_dynamic-slice_fusion
  345.5 2.0 copy.15
  347.5 0.1 broadcast_add_fusion
  347.7 0.7 sub.27
  348.4 3.9 copy.17
  352.3 0.1 broadcast_bitcast_fusion
  353.0 86.1 %reduce-scatter.3.cloned.1.call-done = f32[2048,128]{0,1:T(8,128)} async-done(((f32[2048,512]{0,1:T(8,128)}), f32[2048,128]{0,1:T(8,128)}) %reduce-scatter.3.cloned.1.call-update) | async-done | bytes 1048592 | tf_op jit(solution)/shard_map/reduce_scatter | solution.py:49
  439.1 2.7 fusion.1
  441.9 0.0 reduce-scatter.5.cloned.1.call-start
  441.9 30.3 %all-gather.5.cloned.1.call-done = bf16[2048,512]{0,1:T(8,128)(2,1)} async-done(((bf16[2048,128]{0,1:T(8,128)(2,1)}), bf16[2048,512]{0,1:T(8,128)(2,1)}) %all-gather.5.cloned.1.call-update) | async-done | bytes 2097168 | tf_op jit(solution)/shard_map/all_gather | solution.py:26
  472.2 3.0 multiply_reduce_fusion
  475.3 1.5 multiply_convert_fusion
  476.7 2.2 convolution_bitcast_fusion
  479.0 168.0 %all-reduce.3 = bf16[512,512]{0,1:T(8,128)(2,1)S(1)} all-reduce(f32[512,512]{0,1:T(8,128)} %convolution_bitcast_fusion), channel_id=1, replica_groups=mesh['aux'=4,'pair'=32] {'pair'}, use_global_device_ids=true, to_apply=%region_3.0 | all-reduce | flops 262144 | bytes 1572864 | tf_op jit(solution)/shard_map/psum | solution.py:34
  647.0 1.3 fusion.10
  648.3 0.1 copy-done.1
  648.4 3.3 bitcast_add_fusion
  651.8 66.7 %reduce-scatter.5.cloned.1.call-done = f32[2048,128]{0,1:T(8,128)} async-done(((f32[2048,512]{0,1:T(8,128)}), f32[2048,128]{0,1:T(8,128)}) %reduce-scatter.5.cloned.1.call-update) | async-done | bytes 1048592 | tf_op jit(solution)/shard_map/reduce_scatter | solution.py:49
  718.5 1.8 fusion.3
  720.3 1.0 copy.12
  (23 shorter events, 0.1 us)
Async XLA Ops:
  6.5 166.3 %copy-start = (bf16[2048,512]{1,0:T(8,128)(2,1)S(1)}, bf16[2048,512]{1,0:T(8,128)(2,1)}, u32[]{:S(2)}) copy-start(bf16[2048,512]{1,0:T(8,128)(2,1)} %param.10) | copy-start | bytes 6291460
  6.5 86.3 %copy-start.6 = (bf16[16,384]{1,0:T(8,128)(2,1)S(1)}, bf16[16,384]{1,0:T(8,128)(2,1)}, u32[]{:S(2)}) copy-start(bf16[16,384]{1,0:T(8,128)(2,1)} %param.12) | copy-start | bytes 36868
  6.5 161.8 %all-gather.3.cloned.1.call-start = ((), (), s32[]{:S(2)}) async-start(), calls=%async_computation.2 | async-start | bytes 2621440 | tf_op jit(solution)/shard_map/all_gather | solution.py:26
  7.3 431.9 %reduce-scatter.3.cloned.1.call-start = ((), (), s32[]{:S(2)}) async-start(), calls=%async_computation.3 | async-start | bytes 5242880 | tf_op jit(solution)/shard_map/reduce_scatter | solution.py:49
  168.3 4.5 copy-start.4
  337.7 2.5 copy-start.2
  343.6 4.0 copy-start.7
  343.6 128.6 %all-gather.5.cloned.1.call-start = ((), (), s32[]{:S(2)}) async-start(), calls=%async_computation.4 | async-start | bytes 2621440 | tf_op jit(solution)/shard_map/all_gather | solution.py:26
  348.4 3.9 copy-start.8
  441.9 276.6 %reduce-scatter.5.cloned.1.call-start = ((), (), s32[]{:S(2)}) async-start(), calls=%async_computation.5 | async-start | bytes 5242880 | tf_op jit(solution)/shard_map/reduce_scatter | solution.py:49
  472.2 4.5 copy-start.5
  647.0 1.4 copy-start.1
  651.8 66.7 %copy-start.3 = (bf16[2048,128]{0,1:T(8,128)(2,1)S(1)}, bf16[2048,128]{0,1:T(8,128)(2,1)}, u32[]{:S(2)}) copy-start(bf16[2048,128]{0,1:T(8,128)(2,1)} %copy.15) | copy-start | bytes 1572868
Sparse Core Ops, SparseCore 0:
  9.0 33.8 all-gather.2
  343.7 95.4 reduce-scatter.2
  442.0 30.1 all-gather.4
  651.9 66.5 reduce-scatter.4
where the time goes:
time: 728 us
  blocking collectives  492 us (68%)
  waiting for transfers between devices  184 us (25%)
  matrix products  20.9 us (3%)
  between operations  13.9 us (2%)
  local copies, waits for them, and re-layouts  9.74 us (1%)
  other arithmetic  7.65 us (1%)
    psum x2, blocking collectives, per_device(): gram = lax.psum(gram, 'pair').astype(jnp.bfloat16)  331 us
    reduce_scatter x2, waiting for transfers between devices, per_device(): share = lax.psum_scatter(part, 'aux', scatter_dimension=1, tiled=True)  153 us
    all_gather x1, blocking collectives, per_device(): lax.all_gather(thc_left, 'pair', axis=0, tiled=True)  85.5 us
    all_gather x1, blocking collectives, per_device(): lax.all_gather(thc_right, 'pair', axis=0, tiled=True)  75.5 us
    all_gather x2, waiting for transfers between devices, per_device(): whole = lax.all_gather(local, 'aux', axis=1, tiled=True)  30.3 us
  transfers between devices with their start and end apart: 4, of which 3 were waited for; matrix products, arithmetic and copies ran while one was open for 1% of the time, Pallas kernels for 0%

commit v1 on v0

--- a/solution.py
+++ b/solution.py
@@ -2,8 +2,14 @@
 import jax.numpy as jnp
 from jax import lax
 from jax.sharding import PartitionSpec as P
+from jax.lax import all_gather
 
 ITERS = 2
+
+
+def apply_shapes(inner_x):
+    block_next = jnp.sum(all_gather(inner_x, "pair"), 0)
+    return block_next
 
 
 def per_device(
@@ -31,7 +37,7 @@
         gram = lax.dot_general(
             df_factors, whole, (((0,), (0,)), ((), ())), preferred_element_type=jnp.float32
         )
-        gram = lax.psum(gram, "pair").astype(jnp.bfloat16)
+        gram = apply_shapes(gram).astype(jnp.bfloat16)
         proj = jnp.dot(whole, right, preferred_element_type=jnp.float32).reshape(
             nocc_local, nvirt, right.shape[1]
         )

time: 728 us -> 762 us (1.047)
  blocking collectives: 492 us -> 166 us
  waiting for transfers between devices: 184 us -> 489 us
  local copies, waits for them, and re-layouts: 9.74 us -> 42.4 us
  other arithmetic: 7.65 us -> 26.2 us
    all_gather x0 -> x2, waiting for transfers between devices: none -> 345 us  [apply_shapes(): block_next = jnp.sum(all_gather(inner_x, 'pair'), 0)]
    psum x2 -> x0, blocking collectives: 331 us -> none  [per_device(): gram = lax.psum(gram, 'pair').astype(jnp.bfloat16)]
    reduce_scatter x2, waiting for transfers between devices: 153 us -> 77.7 us  [per_device(): share = lax.psum_scatter(part, 'aux', scatter_dimension=1, tiled=True)]
    all_gather x2, waiting for transfers between devices: 30.3 us -> 64.6 us  [per_device(): whole = lax.all_gather(local, 'aux', axis=1, tiled=True)]
    unnamed x22 -> x21, local copies, waits for them, and re-layouts: 6.15 us -> 38.8 us
    reduce_sum x0 -> x2, other arithmetic: none -> 18.5 us  [apply_shapes(): block_next = jnp.sum(all_gather(inner_x, 'pair'), 0)]
  transfers between devices with their start and end apart: 4 -> 6, of which waited for: 3 -> 6; matrix products, arithmetic and copies ran while one was open for 1% -> 2% of each run, Pallas kernels for 0% -> 0%
where the time goes in v1:
time: 762 us
  waiting for transfers between devices  489 us (64%)
  blocking collectives  166 us (22%)
  local copies, waits for them, and re-layouts  42.4 us (6%)
  other arithmetic  26.2 us (3%)
  matrix products  23.7 us (3%)
  between operations  14.3 us (2%)
    all_gather x2, waiting for transfers between devices, apply_shapes(): block_next = jnp.sum(all_gather(inner_x, 'pair'), 0)  345 us
    all_gather x1, blocking collectives, per_device(): lax.all_gather(thc_left, 'pair', axis=0, tiled=True)  85.5 us
    all_gather x1, blocking collectives, per_device(): lax.all_gather(thc_right, 'pair', axis=0, tiled=True)  80.8 us
    reduce_scatter x2, waiting for transfers between devices, per_device(): share = lax.psum_scatter(part, 'aux', scatter_dimension=1, tiled=True)  77.7 us
    all_gather x2, waiting for transfers between devices, per_device(): whole = lax.all_gather(local, 'aux', axis=1, tiled=True)  64.6 us
    unnamed x21, local copies, waits for them, and re-layouts  38.8 us
    reduce_sum x2, other arithmetic, apply_shapes(): block_next = jnp.sum(all_gather(inner_x, 'pair'), 0)  18.5 us
  transfers between devices with their start and end apart: 6, of which 6 were waited for; matrix products, arithmetic and copies ran while one was open for 2% of the time, Pallas kernels for 0%

profile of v1, /device:TPU:1, one launch (start us, length us, event | category | flops | bytes accessed | tf_op | source)
XLA Modules:
  0.0 761.7 jit_solution(1324210555599846738)
XLA Ops:
  6.5 0.7 all-gather.7.cloned.1.call-update
  7.3 34.3 %all-gather.7.cloned.1.call-done = bf16[2048,512]{1,0:T(8,128)(2,1)} async-done(((bf16[2048,128]{1,0:T(8,128)(2,1)}), bf16[2048,512]{1,0:T(8,128)(2,1)}) %all-gather.7.cloned.1.call-update) | async-done | bytes 2097168 | tf_op jit(solution)/shard_map/all_gather | solution.py:32
  41.6 3.8 fusion.9
  45.5 85.5 %all_gather.29 = bf16[512,384]{1,0:T(8,128)(2,1)S(1)} all-gather(bf16[16,384]{1,0:T(8,128)(2,1)S(1)} %copy-done.4), channel_id=1, replica_groups=mesh['aux'=4,'pair'=32] {'pair'}, dimensions={0}, use_global_device_ids=true | all-gather | bytes 405504 | tf_op jit(solution)/shard_map/all_gather | solution.py:34
  131.1 80.8 %all_gather.30 = bf16[512,384]{1,0:T(8,128)(2,1)S(1)} all-gather(bf16[16,384]{1,0:T(8,128)(2,1)S(1)} %copy-done.5), channel_id=1, replica_groups=mesh['aux'=4,'pair'=32] {'pair'}, dimensions={0}, use_global_device_ids=true | all-gather | bytes 405504 | tf_op jit(solution)/shard_map/all_gather | solution.py:35
  211.9 2.9 multiply_reduce_fusion.1
  214.7 1.5 multiply_convert_fusion.1
  216.2 94.1 %all-gather.11.cloned.1.call-done = f32[16384,512]{1,0:T(8,128)} async-done(((f32[512,512]{1,0:T(8,128)}), f32[16384,512]{1,0:T(8,128)}) %all-gather.11.cloned.1.call-update) | async-done | bytes 33554448 | tf_op jit(solution)/shard_map/all_gather | solution.py:11
  310.3 13.1 %reduce_sum.36 = bf16[512,512]{1,0:T(8,128)(2,1)} reduce(f32[32,512,512]{2,1,0:T(8,128)} %bitcast.44, f32[]{:T(128)} %constant.13.clone.1), dimensions={0}, to_apply=%region_0.0 | reduce | flops 8126464 | bytes 34078724 | tf_op jit(solution)/shard_map/reduce_sum | solution.py:11
  323.4 2.5 fusion.11
  325.9 3.3 bitcast_add_fusion.1
  330.0 1.9 constant_dynamic-slice_fusion
  331.9 2.1 copy.19
  333.9 0.1 broadcast_add_fusion
  334.1 0.7 sub.27
  334.8 4.0 copy.21
  338.8 33.6 %reduce-scatter.3.cloned.1.call-done = f32[2048,128]{0,1:T(8,128)} async-done(((f32[2048,512]{0,1:T(8,128)}), f32[2048,128]{0,1:T(8,128)}) %reduce-scatter.3.cloned.1.call-update) | async-done | bytes 1048592 | tf_op jit(solution)/shard_map/reduce_scatter | solution.py:55
  372.4 2.7 fusion.1
  375.2 30.3 %all-gather.9.cloned.1.call-done = bf16[2048,512]{0,1:T(8,128)(2,1)} async-done(((bf16[2048,128]{0,1:T(8,128)(2,1)}), bf16[2048,512]{0,1:T(8,128)(2,1)}) %all-gather.9.cloned.1.call-update) | async-done | bytes 2097168 | tf_op jit(solution)/shard_map/all_gather | solution.py:32
  405.5 3.8 convolution_bitcast_fusion
  409.3 0.2 reduce-scatter.5.cloned.1.call-start
  409.6 2.9 multiply_reduce_fusion
  412.5 1.5 multiply_convert_fusion
  413.9 251.4 %all-gather.13.cloned.1.call-done = f32[16384,512]{0,1:T(8,128)} async-done(((f32[512,512]{0,1:T(8,128)}), f32[16384,512]{0,1:T(8,128)}) %all-gather.13.cloned.1.call-update) | async-done | bytes 33554448 | tf_op jit(solution)/shard_map/all_gather | solution.py:11
  665.3 32.5 %copy.22 = f32[64,8,32,512]{3,2,1,0:T(8,128)S(1)} copy(f32[64,8,32,512]{3,1,2,0:T(8,128)} %bitcast.45) | data formatting | bytes 67108864
  697.8 5.4 bitcast_reduce_fusion
  703.2 1.3 fusion.10
  704.5 0.1 copy-done.1
  704.6 3.3 bitcast_add_fusion
  707.9 44.2 %reduce-scatter.5.cloned.1.call-done = f32[2048,128]{0,1:T(8,128)} async-done(((f32[2048,512]{0,1:T(8,128)}), f32[2048,128]{0,1:T(8,128)}) %reduce-scatter.5.cloned.1.call-update) | async-done | bytes 1048592 | tf_op jit(solution)/shard_map/reduce_scatter | solution.py:55
  752.1 1.8 fusion.3
  753.9 1.0 copy.16
  (28 shorter events, 0.4 us)
Async XLA Ops:
  6.5 35.1 %copy-start = (bf16[2048,512]{1,0:T(8,128)(2,1)S(1)}, bf16[2048,512]{1,0:T(8,128)(2,1)}, u32[]{:S(2)}) copy-start(bf16[2048,512]{1,0:T(8,128)(2,1)} %param.10) | copy-start | bytes 6291460
  6.5 35.1 %all-gather.7.cloned.1.call-start = ((), (), s32[]{:S(2)}) async-start(), calls=%async_computation.2 | async-start | bytes 2621440 | tf_op jit(solution)/shard_map/all_gather | solution.py:32
  7.3 38.3 %copy-start.4 = (bf16[16,384]{1,0:T(8,128)(2,1)S(1)}, bf16[16,384]{1,0:T(8,128)(2,1)}, u32[]{:S(2)}) copy-start(bf16[16,384]{1,0:T(8,128)(2,1)} %param.11) | copy-start | bytes 36868
  7.3 303.0 %all-gather.11.cloned.1.call-start = ((), (), s32[]{:S(2)}) async-start(), calls=%async_computation.6 | async-start | bytes 34603008 | tf_op jit(solution)/shard_map/all_gather | solution.py:11
  45.4 85.6 %copy-start.5 = (bf16[16,384]{1,0:T(8,128)(2,1)S(1)}, bf16[16,384]{1,0:T(8,128)(2,1)}, u32[]{:S(2)}) copy-start(bf16[16,384]{1,0:T(8,128)(2,1)} %param.12) | copy-start | bytes 36868
  45.5 326.9 %reduce-scatter.3.cloned.1.call-start = ((), (), s32[]{:S(2)}) async-start(), calls=%async_computation.3 | async-start | bytes 5242880 | tf_op jit(solution)/shard_map/reduce_scatter | solution.py:55
  323.4 2.5 copy-start.2
  329.2 0.7 copy-start.7
  329.2 4.7 copy-start.6
  329.2 76.2 %all-gather.9.cloned.1.call-start = ((), (), s32[]{:S(2)}) async-start(), calls=%async_computation.4 | async-start | bytes 2621440 | tf_op jit(solution)/shard_map/all_gather | solution.py:32
  375.1 290.1 %all-gather.13.cloned.1.call-start = ((), (), s32[]{:S(2)}) async-start(), calls=%async_computation.7 | async-start | bytes 34603008 | tf_op jit(solution)/shard_map/all_gather | solution.py:11
  409.3 342.8 %reduce-scatter.5.cloned.1.call-start = ((), (), s32[]{:S(2)}) async-start(), calls=%async_computation.5 | async-start | bytes 5242880 | tf_op jit(solution)/shard_map/reduce_scatter | solution.py:55
  703.2 1.4 copy-start.1
  707.9 44.2 %copy-start.3 = (bf16[2048,128]{0,1:T(8,128)(2,1)S(1)}, bf16[2048,128]{0,1:T(8,128)(2,1)}, u32[]{:S(2)}) copy-start(bf16[2048,128]{0,1:T(8,128)(2,1)} %copy.19) | copy-start | bytes 1572868
Sparse Core Ops, SparseCore 0:
  9.0 32.5 all-gather.6
  45.6 264.6 all-gather.10
  329.3 43.0 reduce-scatter.2
  375.3 30.1 all-gather.8
  409.4 255.7 all-gather.12
  708.1 43.9 reduce-scatter.4
